TPU v7x, 32 devices: a whole 2x2x4 slice. The times are simulated.
32 devices in a mesh: grp: 4 (over z), seq: 8 (over y, x, core).
Axes of the slice: x: 2, y: 2, z: 4, core: 2. Of those that a mesh axis runs over, the one named last changes fastest.
Arguments:
- hidden_in: bfloat16 [24, 4096], P(None, ('grp', 'seq')), may hold values from -6 to 6
- norm_gain: float32 [4096], replicated, may hold values from 0.5 to 1.5
- w_ssm_in: bfloat16 [4096, 8192], P(None, ('grp', 'seq')), may hold values from -0.09375 to 0.09375
- w_ssm_gate: bfloat16 [4096, 8192], P(None, ('grp', 'seq')), may hold values from -0.09375 to 0.09375
- conv_weight: float32 [4, 8192], P(None, ('grp', 'seq')), may hold values from -3 to 3
- conv_bias: float32 [8192], P(('grp', 'seq')), may hold values from -0.5 to 0.5
- conv_state: bfloat16 [24, 3, 8192], P(None, None, ('grp', 'seq')), may hold values from -6 to 6
- w_state_proj: bfloat16 [8192, 288], P(('grp', 'seq')), may hold values from -0.0625 to 0.0625
- w_step: bfloat16 [256, 8192], P(None, ('grp', 'seq')), may hold values from -0.375 to 0.375
- step_bias: float32 [8192], P(('grp', 'seq')), may hold values from -4 to -1
- log_decay: float32 [16, 8192], P(None, ('grp', 'seq')), may hold values from 0 to 2.7
- skip_gain: float32 [8192], P(('grp', 'seq')), may hold values from 0.5 to 1.5
- ssm_state: float32 [24, 16, 8192], P(None, None, ('grp', 'seq')), may hold values from -6 to 6
- w_ssm_out: bfloat16 [8192, 4096], P(('grp', 'seq')), may hold values from -0.125 to 0.125
- w_query: bfloat16 [4096, 2048], P(None, 'grp'), may hold values from -6 to 6
- key_projection: bfloat16 [4096, 1024], P(None, 'grp'), may hold values from -0.09375 to 0.09375
- value_projection: bfloat16 [4096, 1024], P(None, 'grp'), may hold values from -0.09375 to 0.09375
- w_attn_out: bfloat16 [2048, 4096], P('grp', 'seq'), may hold values from -0.125 to 0.125
- w_mlp_gate: bfloat16 [4096, 14336], P(None, ('grp', 'seq')), may hold values from -0.09375 to 0.09375
- w_mlp_up: bfloat16 [4096, 14336], P(None, ('grp', 'seq')), may hold values from -0.09375 to 0.09375
- w_mlp_down: bfloat16 [14336, 4096], P(('grp', 'seq')), may hold values from -0.09375 to 0.09375
- cached_inputs: bfloat16 [24, 512, 4096], P('seq'), may hold values from -6 to 6
- window_lengths: int32 [24], replicated, may hold values from 1 to 512, as said below
Outputs:
- hidden_out: bfloat16 [24, 4096], P(None, ('grp', 'seq'))
- state_out: float32 [24, 16, 8192], P(None, None, ('grp', 'seq'))
Inputs may be any that keep to these rules, and one draw needn't show every extreme that they name: `window_lengths`: every sequence has at least one valid cached position, and some sequence fills the whole window of 512.
All inputs are finite; a program needn't handle non-finite values.
Results may differ from a plain program's by a relative error of at most 0.012.
The roundings to bfloat16 on the way count: a program that leaves them out, or rounds other values in their place, can miss the bound.
Values may be sent and summed in bfloat16 or wider, within the bound.
A program may use at most 128 MiB of HBM per device.

v0:
```python
import jax
import jax.numpy as jnp
from jax import lax
from jax.sharding import PartitionSpec as P

HEAD_SIZE = 128


epsilon = 1e-05
rope_base = 10000.0


def apply_rotary(head_values, positions):
    half_dim = head_values.shape[-1] // 2
    frequency = rope_base ** (
        -(jnp.arange(half_dim, dtype=jnp.float32) * 2.0) / head_values.shape[-1]
    )
    angles = positions[..., None, None] * frequency
    cosine = jnp.cos(angles)
    sine_part = jnp.sin(angles)
    front_half = head_values[..., :half_dim]
    back_half = head_values[..., half_dim:]
    return jnp.concatenate(
        [front_half * cosine - back_half * sine_part, back_half * cosine + front_half * sine_part],
        axis=-1,
    )


def per_device(
    hidden_in,
    norm_gain,
    w_ssm_in,
    w_ssm_gate,
    conv_weight,
    conv_bias,
    conv_state,
    w_state_proj,
    w_step,
    step_bias,
    log_decay,
    skip_gain,
    ssm_state,
    w_ssm_out,
    w_query,
    key_projection,
    value_projection,
    w_attn_out,
    w_mlp_gate,
    w_mlp_up,
    w_mlp_down,
    cached_inputs,
    window_lengths,
):
    batch_rows = hidden_in.shape[0]
    model_width = norm_gain.shape[0]
    hidden_f = hidden_in.astype(jnp.float32)
    raw_full = lax.all_gather(hidden_in, ("grp", "seq"), axis=1, tiled=True).astype(jnp.float32)
    row_scale = lax.rsqrt(jnp.mean(raw_full * raw_full, axis=1, keepdims=True) + epsilon)
    normed_input = (raw_full * row_scale * norm_gain).astype(jnp.bfloat16)
    ssm_input = jnp.dot(normed_input, w_ssm_in, preferred_element_type=jnp.float32).astype(
        jnp.bfloat16
    )
    gate_input = jnp.dot(normed_input, w_ssm_gate, preferred_element_type=jnp.float32)
    past_inputs = conv_state.astype(jnp.float32)
    conv_sum = (
        conv_bias
        + jnp.sum(past_inputs * conv_weight[:-1][None], axis=1)
        + conv_weight[-1] * lax.optimization_barrier(ssm_input).astype(jnp.float32)
    )
    conv_out = jax.nn.silu(conv_sum)
    rank_size = w_step.shape[0]
    state_size = log_decay.shape[0]
    low_rank = lax.psum(
        jnp.dot(conv_out.astype(jnp.bfloat16), w_state_proj, preferred_element_type=jnp.float32),
        ("grp", "seq"),
    )
    step_low = low_rank[:, :rank_size].astype(jnp.bfloat16)
    input_map = low_rank[:, rank_size : rank_size + state_size]
    output_map = low_rank[:, rank_size + state_size :]
    step_size = jax.nn.softplus(
        jnp.dot(step_low, w_step, preferred_element_type=jnp.float32) + step_bias
    )
    decay_rate = jnp.exp(log_decay)
    state_out = (
        jnp.exp(-step_size[:, None, :] * decay_rate[None]) * ssm_state
        + step_size[:, None, :] * input_map[:, :, None] * conv_out[:, None, :]
    )
    ssm_mixed = jnp.sum(state_out * output_map[:, :, None], axis=1) + skip_gain * conv_out
    ssm_gated = (ssm_mixed * jax.nn.silu(gate_input)).astype(jnp.bfloat16)
    ssm_term = jnp.dot(ssm_gated, w_ssm_out, preferred_element_type=jnp.float32)
    ssm_summed = lax.psum_scatter(ssm_term, ("grp", "seq"), scatter_dimension=1, tiled=True)
    gate_act = jnp.dot(normed_input, w_mlp_gate, preferred_element_type=jnp.float32)
    up_act = jnp.dot(normed_input, w_mlp_up, preferred_element_type=jnp.float32)
    mlp_hidden = (jax.nn.silu(gate_act) * up_act).astype(jnp.bfloat16)
    mlp_term = jnp.dot(mlp_hidden, w_mlp_down, preferred_element_type=jnp.float32)
    own_seqs = cached_inputs.shape[0]
    window_size = cached_inputs.shape[1]
    seq_start = lax.axis_index("seq") * own_seqs
    normed_own = lax.dynamic_slice_in_dim(normed_input, seq_start, own_seqs, 0)
    lengths_own = lax.dynamic_slice_in_dim(window_lengths, seq_start, own_seqs, 0)
    heads_here = w_query.shape[1] // HEAD_SIZE
    kv_here = key_projection.shape[1] // HEAD_SIZE
    heads_per_group = heads_here // kv_here
    attention_scale = HEAD_SIZE ** (-0.5)
    fresh_position = lengths_own.astype(jnp.float32)
    query = apply_rotary(
        jnp.dot(normed_own, w_query, preferred_element_type=jnp.float32).reshape(
            own_seqs, heads_here, HEAD_SIZE
        ),
        fresh_position,
    ).astype(jnp.bfloat16)
    fresh_key = apply_rotary(
        jnp.dot(normed_own, key_projection, preferred_element_type=jnp.float32).reshape(
            own_seqs, kv_here, HEAD_SIZE
        ),
        fresh_position,
    ).astype(jnp.bfloat16)
    fresh_value = (
        jnp.dot(normed_own, value_projection, preferred_element_type=jnp.float32)
        .astype(jnp.bfloat16)
        .reshape(own_seqs, kv_here, HEAD_SIZE)
    )
    flat_inputs = cached_inputs.reshape(own_seqs * window_size, model_width)
    slot_ids = jnp.arange(window_size, dtype=jnp.int32)
    positions = jnp.broadcast_to(slot_ids[None, :], (own_seqs, window_size)).astype(jnp.float32)
    window_key_rows = jnp.dot(
        flat_inputs, key_projection, preferred_element_type=jnp.float32
    ).reshape(own_seqs, window_size, kv_here, HEAD_SIZE)
    window_key_rows = apply_rotary(window_key_rows, positions).astype(jnp.bfloat16)
    window_value_rows = (
        jnp.dot(flat_inputs, value_projection, preferred_element_type=jnp.float32)
        .astype(jnp.bfloat16)
        .reshape(own_seqs, window_size, kv_here, HEAD_SIZE)
    )
    grouped_query = query.astype(jnp.float32).reshape(own_seqs, kv_here, heads_per_group, HEAD_SIZE)
    scores = (
        jnp.einsum("bkgd,bpkd->bkgp", grouped_query, window_key_rows.astype(jnp.float32))
        * attention_scale
    )
    fresh_score = (
        jnp.einsum("ynow,ynw->yno", grouped_query, fresh_key.astype(jnp.float32)) * attention_scale
    )
    is_valid = (slot_ids[None, :] < lengths_own[:, None])[:, None, None, :]
    scores = jnp.where(is_valid, scores, -1e30)
    joint_max = jnp.maximum(jnp.max(scores, axis=-1), fresh_score)
    weights = jnp.where(is_valid, jnp.exp(scores - joint_max[..., None]), 0.0)
    weight_new = jnp.exp(fresh_score - joint_max)
    joint_total = jnp.sum(weights, axis=-1) + weight_new
    joint_sum = (
        jnp.einsum("bkgp,bpkd->bkgd", weights, window_value_rows.astype(jnp.float32))
        + weight_new[..., None] * fresh_value.astype(jnp.float32)[:, :, None, :]
    )
    attended_own = (
        (joint_sum / joint_total[..., None])
        .reshape(own_seqs, heads_here * HEAD_SIZE)
        .astype(jnp.bfloat16)
    )
    attended = lax.all_gather(attended_own, "seq", axis=0, tiled=True)
    attn_cols = jnp.dot(attended, w_attn_out, preferred_element_type=jnp.float32)
    col_start = lax.axis_index("seq") * w_attn_out.shape[1]
    attn_term = lax.dynamic_update_slice(
        jnp.zeros((batch_rows, model_width), jnp.float32), attn_cols, (jnp.int32(0), col_start)
    )
    other_terms = mlp_term + attn_term
    summed = ssm_summed + lax.psum_scatter(
        other_terms, ("grp", "seq"), scatter_dimension=1, tiled=True
    )
    hidden_out = (hidden_f + summed).astype(jnp.bfloat16)
    return (hidden_out, state_out)


def solution(mesh):
    placed = (
        P(None, ("grp", "seq")),
        P(),
        P(None, ("grp", "seq")),
        P(None, ("grp", "seq")),
        P(None, ("grp", "seq")),
        P(("grp", "seq")),
        P(None, None, ("grp", "seq")),
        P(("grp", "seq"), None),
        P(None, ("grp", "seq")),
        P(("grp", "seq")),
        P(None, ("grp", "seq")),
        P(("grp", "seq")),
        P(None, None, ("grp", "seq")),
        P(("grp", "seq"), None),
        P(None, "grp"),
        P(None, "grp"),
        P(None, "grp"),
        P("grp", "seq"),
        P(None, ("grp", "seq")),
        P(None, ("grp", "seq")),
        P(("grp", "seq"), None),
        P("seq", None, None),
        P(),
    )
    return jax.shard_map(
        per_device,
        mesh=mesh,
        in_specs=placed,
        out_specs=(P(None, ("grp", "seq")), P(None, None, ("grp", "seq"))),
        check_vma=False,
    )
```

profile of v0, /device:TPU:0, one launch (start us, length us, event | category | flops | bytes accessed | tf_op | source)
XLA Modules:
  0.0 289.1 jit_solution(317169863830582743)
XLA Ops:
  7.3 44.2 %all_gather.6 = bf16[24,4096]{1,0:T(8,128)(2,1)S(1)} all-gather(bf16[24,128]{1,0:T(8,128)(2,1)} %param.23), channel_id=1, replica_groups=mesh['grp'=4,'seq'=8] {'grp','seq'}, dimensions={1}, use_global_device_ids=true | all-gather | bytes 202752 | tf_op jit(solution)/shard_map/all_gather | solution.py:57
  51.4 0.2 fusion.13
  51.6 0.8 fusion.15
  52.5 2.8 fusion.25
  55.3 0.1 fusion.42
  55.5 0.1 multiply_cosine_fusion.1
  55.6 0.5 multiply_cosine_fusion
  56.1 2.0 fusion.23
  58.1 4.1 %copy.38 = bf16[256,4096]{1,0:T(8,128)(2,1)} copy(bf16[256,4096]{0,1:T(8,128)(2,1)} %bitcast.38) | data formatting | bytes 4194304 | tf_op jit(solution)/shard_map/dot_general | solution.py:126
  62.3 0.1 subtract_convert_fusion.2
  62.3 7.1 %fusion = f32[3,512,2,128]{1,3,2,0:T(8,128)S(1)} fusion(bf16[2,128,4096,1]{2,1,0,3:T(8,128)(2,1)} %bitcast.39, bf16[3,512,4096]{2,1,0:T(8,128)(2,1)} %param.44), kind=kOutput, calls=%fused_computation | convolution fusion | flops 3221225472 | bytes 16252928 | tf_op jit(solution)/shard_map/dot_general | solution.py:126
  69.5 0.1 maximum_bitcast_fusion
  69.6 0.3 subtract_convert_fusion
  69.9 0.2 fusion.32
  70.1 0.3 fusion.44
  70.5 0.2 fusion.31
  70.7 0.4 fusion.8
  71.1 7.4 %convolution_convert_fusion = bf16[1536,256]{1,0:T(8,128)(2,1)} fusion(bf16[1536,4096]{1,0:T(8,128)(2,1)} %bitcast.48, bf16[4096,256]{1,0:T(8,128)(2,1)S(1)} %copy-done), kind=kOutput, calls=%fused_computation.3 | convolution fusion | flops 3221618688 | bytes 15466496 | tf_op jit(solution)/shard_map/dot_general | solution.py:131
  78.4 2.0 reshape.155
  80.5 0.3 fusion.7
  80.8 7.0 %all-gather = bf16[8,3,512]{2,1,0:T(4,128)(2,1)S(1)} all-gather(bf16[1,3,512]{2,1,0:T(4,128)(2,1)S(1)} %reshape.157), channel_id=1, replica_groups=mesh['grp'=4,'seq'=8] {'seq'}, dimensions={0}, use_global_device_ids=true | all-gather | bytes 27648 | tf_op jit(solution)/shard_map/all_gather | solution.py:158
  87.8 3.1 %fusion.48 = f32[24,448]{1,0:T(8,128)S(1)} fusion(bf16[24,4096]{1,0:T(8,128)(2,1)S(1)} %fusion.15, bf16[4096,448]{0,1:T(8,128)(2,1)} %param.41), kind=kOutput, calls=%fused_computation.85 | convolution fusion | flops 88080384 | bytes 3909632 | tf_op jit(solution)/shard_map/dot_general | solution.py:92
  91.0 2.1 convolution_convert_fusion.1
  93.2 0.2 fusion.28
  93.4 38.3 %psum.7 = f32[24,288]{1,0:T(8,128)S(1)} all-reduce(f32[24,288]{1,0:T(8,128)S(1)} %fusion.28), channel_id=1, replica_groups=mesh['grp'=4,'seq'=8] {'grp','seq'}, use_global_device_ids=true, to_apply=%region_2.3 | all-reduce | flops 6912 | bytes 55296 | tf_op jit(solution)/shard_map/psum | solution.py:73
  131.8 0.2 fusion.45
  132.0 5.1 %fusion.4 = f32[24,4096]{1,0:T(8,128)S(1)} fusion(bf16[448,4096]{1,0:T(8,128)(2,1)} %param.43, bf16[24,4096]{1,0:T(8,128)(2,1)S(1)} %fusion.15, bf16[4096,448]{0,1:T(8,128)(2,1)} %param.42, f32[24,448]{1,0:T(8,128)S(1)} %fusion.48), kind=kOutput, calls=%fused_computation.8 | convolution fusion | flops 176225280 | bytes 7972864 | tf_op jit(solution)/shard_map/dot_general | solution.py:95
  137.1 0.2 fusion.2
  137.3 1.9 multiply_reduce_fusion
  139.3 4.3 %convolution_add_fusion = f32[24,4096]{1,0:T(8,128)} fusion(f32[24,4096]{1,0:T(8,128)S(1)} %fusion.2, bf16[256,4096]{1,0:T(8,128)(2,1)} %param.36, f32[24,256]{1,0:T(8,128)S(1)} %get-tuple-element.2, f32[24,256]{1,0:T(8,128)S(1)} %divide_multiply_fusion, f32[256]{0:T(256)S(1)} %copy-done.10, bf16[24,4096]{1,0:T(8,128)(2,1)S(1)} %fusion.15, ...), kind=kOutput, calls=%fused_computation.2 | convolution fusion | flops 100810752 | bytes 5227520 | tf_op jit(solution)/shard_map/dot_general | solution.py:90
  143.6 137.4 %reduce-scatter.2.cloned.1.call-done = f32[24,128]{1,0:T(8,128)} async-done(((f32[24,4096]{1,0:T(8,128)}), f32[24,128]{1,0:T(8,128)}) %reduce-scatter.2.cloned.1.call-update) | async-done | bytes 12304 | tf_op jit(solution)/shard_map/reduce_scatter | solution.py:91
  280.9 1.3 add_convert_fusion.1
  (43 shorter events, 0.6 us)
Async XLA Ops:
  7.2 63.5 %copy-start = (bf16[4096,256]{1,0:T(8,128)(2,1)S(1)}, bf16[4096,256]{1,0:T(8,128)(2,1)}, u32[]{:S(2)}) copy-start(bf16[4096,256]{1,0:T(8,128)(2,1)} %param.39) | copy-start | bytes 6291460
  7.2 273.8 %reduce-scatter.2.cloned.1.call-start = ((), (), s32[]{:S(2)}) async-start(), calls=%async_computation.1 | async-start | bytes 405504 | tf_op jit(solution)/shard_map/reduce_scatter | solution.py:91
  52.4 2.9 copy-start.11
  90.9 2.2 copy-start.7
  90.9 2.2 copy-start.4
  91.0 2.2 copy-start.8
  91.0 2.2 copy-start.2
  91.0 40.8 %copy-start.6 = (f32[16,256]{1,0:T(8,128)S(1)}, f32[16,256]{1,0:T(8,128)}, u32[]{:S(2)}) copy-start(f32[16,256]{1,0:T(8,128)} %param.33) | copy-start | bytes 49156
  91.0 40.8 %copy-start.3 = (bf16[256,256]{1,0:T(8,128)(2,1)S(1)}, bf16[256,256]{1,0:T(8,128)(2,1)}, u32[]{:S(2)}) copy-start(bf16[256,256]{1,0:T(8,128)(2,1)} %param.31) | copy-start | bytes 393220
  91.0 40.8 %copy-start.9 = (f32[256]{0:T(256)S(1)}, f32[256]{0:T(256)}, u32[]{:S(2)}) copy-start(f32[256]{0:T(256)} %param.32) | copy-start | bytes 3076
  132.0 5.1 %copy-start.1 = (bf16[512,512]{1,0:T(8,128)(2,1)S(1)}, bf16[512,512]{1,0:T(8,128)(2,1)}, u32[]{:S(2)}) copy-start(bf16[512,512]{1,0:T(8,128)(2,1)} %param.40) | copy-start | bytes 1572868
  132.0 7.2 %copy-start.10 = (f32[256]{0:T(256)S(1)}, f32[256]{0:T(256)}, u32[]{:S(2)}) copy-start(f32[256]{0:T(256)} %param.34) | copy-start | bytes 3076
  139.3 141.7 %copy-start.5 = (bf16[24,128]{1,0:T(8,128)(2,1)S(1)}, bf16[24,128]{1,0:T(8,128)(2,1)}, u32[]{:S(2)}) copy-start(bf16[24,128]{1,0:T(8,128)(2,1)} %param.23) | copy-start | bytes 18436
Sparse Core Ops, SparseCore 0:
  143.7 137.2 reduce-scatter.1
where the time goes:
time: 290 us; the launch traced here: 289 us
  waiting for transfers between devices  137 us (47%)
  blocking collectives  89.5 us (31%)
  matrix products  35.6 us (12%)
  between operations  14.3 us (5%)
  local copies, waits for them, and re-layouts  6.37 us (2%)
  other arithmetic  5.87 us (2%)
    reduce_scatter x1, waiting for transfers between devices, per_device(): lax.psum_scatter(ssm_term, ('grp', 'seq'), scatter_dimension=1, tiled=True)  137 us
    all_gather x1, blocking collectives, per_device(): lax.all_gather(hidden_in, ('grp', 'seq'), axis=1, tiled=True)  44.2 us
    psum x1, blocking collectives, per_device(): lax.psum(jnp.dot(conv_out.astype(jnp.bfloat16), w_state_proj, preferred_e...  38.3 us
    dot_general x1, matrix products, per_device(): jnp.dot(flat_inputs, value_projection, preferred_element_type=jnp.float32)  7.38 us
    dot_general x1, matrix products, per_device(): jnp.dot(flat_inputs, key_projection, preferred_element_type=jnp.float32)  7.13 us
    all_gather x1, blocking collectives, per_device(): attended = lax.all_gather(attended_own, 'seq', axis=0, tiled=True)  7.02 us
  transfers between devices with their start and end apart: 1, of which 1 were waited for; matrix products, arithmetic and copies ran while one was open for 0% of the time, Pallas kernels for 0%

commit v1 on v0

--- a/solution.py
+++ b/solution.py
@@ -1,9 +1,15 @@
+import functools
+
 import jax
 import jax.numpy as jnp
 from jax import lax
+from jax.experimental import pallas as pl
+from jax.experimental.pallas import tpu as pltpu
 from jax.sharding import PartitionSpec as P
 
 HEAD_SIZE = 128
+MESH = pl.DeviceIdType.MESH
+VMEM_SPEC = pl.BlockSpec(memory_space=pltpu.VMEM)
 
 
 epsilon = 1e-05
@@ -26,7 +32,273 @@
     )
 
 
+def my_index(seq_size):
+    return lax.axis_index("grp") * seq_size + lax.axis_index("seq")
+
+
+def device_at(index, seq_size):
+    return (index // seq_size, index % seq_size)
+
+
+def meet_all(devices, seq_size):
+    me = my_index(seq_size)
+    barrier = pltpu.get_barrier_semaphore()
+
+    def greet(k, carry):
+        pl.semaphore_signal(
+            barrier,
+            inc=1,
+            device_id=device_at(lax.rem(me + k, devices), seq_size),
+            device_id_type=MESH,
+        )
+        return carry
+
+    lax.fori_loop(1, devices, greet, 0)
+    pl.semaphore_wait(barrier, devices - 1)
+
+
+def each_peer(devices, action):
+    def step(k, carry):
+        action(k)
+        return carry
+
+    lax.fori_loop(1, devices, step, 0)
+
+
+def norm_gather_kernel(devices, seq_size, x_ref, gain_ref, out_ref, buf, send_sem, recv_sem):
+    me = my_index(seq_size)
+    width = x_ref.shape[1]
+    meet_all(devices, seq_size)
+
+    def copy_for(k):
+        return pltpu.make_async_remote_copy(
+            src_ref=x_ref,
+            dst_ref=buf.at[me],
+            send_sem=send_sem.at[k],
+            recv_sem=recv_sem.at[k],
+            device_id=device_at(lax.rem(me + k, devices), seq_size),
+            device_id_type=MESH,
+        )
+
+    each_peer(devices, lambda k: copy_for(k).start())
+    buf[me] = x_ref[...]
+    each_peer(devices, lambda k: copy_for(k).wait())
+    total = jnp.zeros(x_ref.shape, jnp.float32)
+    for d in range(devices):
+        block = buf[d].astype(jnp.float32)
+        total = total + block * block
+    scale = lax.rsqrt(
+        jnp.sum(total, axis=1, keepdims=True) * (1.0 / (devices * width)) + epsilon
+    )
+    for d in range(devices):
+        cols = slice(d * width, (d + 1) * width)
+        out_ref[:, cols] = (buf[d].astype(jnp.float32) * scale * gain_ref[:, cols]).astype(
+            jnp.bfloat16
+        )
+
+
+def norm_gather(devices, seq_size, hidden_in, norm_gain):
+    rows, width = hidden_in.shape
+    return pl.pallas_call(
+        functools.partial(norm_gather_kernel, devices, seq_size),
+        out_shape=jax.ShapeDtypeStruct((rows, devices * width), jnp.bfloat16),
+        in_specs=[VMEM_SPEC] * 2,
+        out_specs=VMEM_SPEC,
+        scratch_shapes=[
+            pltpu.VMEM((devices, rows, width), jnp.bfloat16),
+            pltpu.SemaphoreType.DMA((devices,)),
+            pltpu.SemaphoreType.DMA((devices,)),
+        ],
+        compiler_params=pltpu.CompilerParams(collective_id=0, has_side_effects=True),
+    )(hidden_in, norm_gain.reshape(1, -1))
+
+
+def sum_gather_kernel(
+    devices,
+    seq_size,
+    part_ref,
+    att_ref,
+    out_ref,
+    att_out_ref,
+    split,
+    landed,
+    reduced,
+    full,
+    att_buf,
+    send_sem,
+    recv_sem,
+    send_all_sem,
+    recv_all_sem,
+    att_send_sem,
+    att_recv_sem,
+):
+    me = my_index(seq_size)
+    group = lax.axis_index("grp")
+    place = lax.axis_index("seq")
+    owners, each = split.shape[0], split.shape[1]
+    own_rows = att_ref.shape[0]
+    for r in range(owners):
+        split[r] = part_ref[r * each : (r + 1) * each, :]
+    meet_all(devices, seq_size)
+
+    def peer(k):
+        return lax.rem(me + k, devices)
+
+    def part_copy(k):
+        return pltpu.make_async_remote_copy(
+            src_ref=split.at[lax.rem(peer(k), owners)],
+            dst_ref=landed.at[me],
+            send_sem=send_sem.at[k],
+            recv_sem=recv_sem.at[k],
+            device_id=device_at(peer(k), seq_size),
+            device_id_type=MESH,
+        )
+
+    def full_copy(k):
+        return pltpu.make_async_remote_copy(
+            src_ref=reduced,
+            dst_ref=full.at[lax.rem(me, owners)],
+            send_sem=send_all_sem.at[k],
+            recv_sem=recv_all_sem.at[k],
+            device_id=device_at(peer(k), seq_size),
+            device_id_type=MESH,
+        )
+
+    def att_copy(k):
+        return pltpu.make_async_remote_copy(
+            src_ref=att_ref,
+            dst_ref=att_buf.at[place],
+            send_sem=att_send_sem.at[k],
+            recv_sem=att_recv_sem.at[k],
+            device_id=(group, lax.rem(place + k, seq_size)),
+            device_id_type=MESH,
+        )
+
+    def start_part(k):
+        @pl.when(peer(k) < owners)
+        def _():
+            part_copy(k).start()
+
+    each_peer(devices, start_part)
+    each_peer(seq_size, lambda k: att_copy(k).start())
+    att_buf[place] = att_ref[...]
+
+    @pl.when(me < owners)
+    def _():
+        landed[me] = split[me]
+        each_peer(devices, lambda k: part_copy(k).wait_recv())
+        total = landed[0]
+        for d in range(1, devices):
+            total = total + landed[d]
+        reduced[...] = total
+        full[me] = total
+        each_peer(devices, lambda k: full_copy(k).start())
+
+    def end_part(k):
+        @pl.when(peer(k) < owners)
+        def _():
+            part_copy(k).wait_send()
+
+    each_peer(devices, end_part)
+    each_peer(seq_size, lambda k: att_copy(k).wait())
+    for s in range(seq_size):
+        att_out_ref[s * own_rows : (s + 1) * own_rows, :] = att_buf[s]
+
+    def end_full(k):
+        @pl.when(lax.rem(me + devices - k, devices) < owners)
+        def _():
+            full_copy(k).wait_recv()
+
+    each_peer(devices, end_full)
+
+    @pl.when(me < owners)
+    def _():
+        each_peer(devices, lambda k: full_copy(k).wait_send())
+
+    for r in range(owners):
+        out_ref[r * each : (r + 1) * each, :] = full[r]
+
+
+def sum_gather(devices, seq_size, part, att):
+    rows, width = part.shape
+    each = -(-rows // devices)
+    while rows % each:
+        each += 1
+    owners = rows // each
+    dma = pltpu.SemaphoreType.DMA
+    return pl.pallas_call(
+        functools.partial(sum_gather_kernel, devices, seq_size),
+        out_shape=(
+            jax.ShapeDtypeStruct((rows, width), jnp.float32),
+            jax.ShapeDtypeStruct((seq_size * att.shape[0], att.shape[1]), jnp.float32),
+        ),
+        in_specs=[VMEM_SPEC] * 2,
+        out_specs=(VMEM_SPEC, VMEM_SPEC),
+        scratch_shapes=[
+            pltpu.VMEM((owners, each, width), jnp.float32),
+            pltpu.VMEM((devices, each, width), jnp.float32),
+            pltpu.VMEM((each, width), jnp.float32),
+            pltpu.VMEM((owners, each, width), jnp.float32),
+            pltpu.VMEM((seq_size,) + att.shape, jnp.float32),
+            dma((devices,)),
+            dma((devices,)),
+            dma((devices,)),
+            dma((devices,)),
+            dma((seq_size,)),
+            dma((seq_size,)),
+        ],
+        compiler_params=pltpu.CompilerParams(collective_id=1, has_side_effects=True),
+    )(part, att)
+
+
+def scatter_sum_kernel(
+    devices, seq_size, term_ref, hidden_ref, out_ref, outgoing, landed, send_sem, recv_sem
+):
+    me = my_index(seq_size)
+    width = hidden_ref.shape[1]
+    for d in range(devices):
+        outgoing[d] = term_ref[:, d * width : (d + 1) * width].astype(jnp.bfloat16)
+    meet_all(devices, seq_size)
+
+    def copy_for(k):
+        return pltpu.make_async_remote_copy(
+            src_ref=outgoing.at[lax.rem(me + k, devices)],
+            dst_ref=landed.at[me],
+            send_sem=send_sem.at[k],
+            recv_sem=recv_sem.at[k],
+            device_id=device_at(lax.rem(me + k, devices), seq_size),
+            device_id_type=MESH,
+        )
+
+    each_peer(devices, lambda k: copy_for(k).start())
+    landed[me] = outgoing[me]
+    each_peer(devices, lambda k: copy_for(k).wait())
+    total = landed[0].astype(jnp.float32)
+    for d in range(1, devices):
+        total = total + landed[d].astype(jnp.float32)
+    out_ref[...] = (hidden_ref[...].astype(jnp.float32) + total).astype(jnp.bfloat16)
+
+
+def scatter_sum(devices, seq_size, term, hidden_in):
+    rows, width = hidden_in.shape
+    return pl.pallas_call(
+        functools.partial(scatter_sum_kernel, devices, seq_size),
+        out_shape=jax.ShapeDtypeStruct((rows, width), jnp.bfloat16),
+        in_specs=[VMEM_SPEC] * 2,
+        out_specs=VMEM_SPEC,
+        scratch_shapes=[
+            pltpu.VMEM((devices, rows, width), jnp.bfloat16),
+            pltpu.VMEM((devices, rows, width), jnp.bfloat16),
+            pltpu.SemaphoreType.DMA((devices,)),
+            pltpu.SemaphoreType.DMA((devices,)),
+        ],
+        compiler_params=pltpu.CompilerParams(collective_id=2, has_side_effects=True),
+    )(term, hidden_in)
+
+
 def per_device(
+    devices,
+    seq_size,
     hidden_in,
     norm_gain,
     w_ssm_in,
@@ -53,10 +325,7 @@
 ):
     batch_rows = hidden_in.shape[0]
     model_width = norm_gain.shape[0]
-    hidden_f = hidden_in.astype(jnp.float32)
-    raw_full = lax.all_gather(hidden_in, ("grp", "seq"), axis=1, tiled=True).astype(jnp.float32)
-    row_scale = lax.rsqrt(jnp.mean(raw_full * raw_full, axis=1, keepdims=True) + epsilon)
-    normed_input = (raw_full * row_scale * norm_gain).astype(jnp.bfloat16)
+    normed_input = norm_gather(devices, seq_size, hidden_in, norm_gain)
     ssm_input = jnp.dot(normed_input, w_ssm_in, preferred_element_type=jnp.float32).astype(
         jnp.bfloat16
     )
@@ -70,29 +339,9 @@
     conv_out = jax.nn.silu(conv_sum)
     rank_size = w_step.shape[0]
     state_size = log_decay.shape[0]
-    low_rank = lax.psum(
-        jnp.dot(conv_out.astype(jnp.bfloat16), w_state_proj, preferred_element_type=jnp.float32),
-        ("grp", "seq"),
-    )
-    step_low = low_rank[:, :rank_size].astype(jnp.bfloat16)
-    input_map = low_rank[:, rank_size : rank_size + state_size]
-    output_map = low_rank[:, rank_size + state_size :]
-    step_size = jax.nn.softplus(
-        jnp.dot(step_low, w_step, preferred_element_type=jnp.float32) + step_bias
-    )
-    decay_rate = jnp.exp(log_decay)
-    state_out = (
-        jnp.exp(-step_size[:, None, :] * decay_rate[None]) * ssm_state
-        + step_size[:, None, :] * input_map[:, :, None] * conv_out[:, None, :]
-    )
-    ssm_mixed = jnp.sum(state_out * output_map[:, :, None], axis=1) + skip_gain * conv_out
-    ssm_gated = (ssm_mixed * jax.nn.silu(gate_input)).astype(jnp.bfloat16)
-    ssm_term = jnp.dot(ssm_gated, w_ssm_out, preferred_element_type=jnp.float32)
-    ssm_summed = lax.psum_scatter(ssm_term, ("grp", "seq"), scatter_dimension=1, tiled=True)
-    gate_act = jnp.dot(normed_input, w_mlp_gate, preferred_element_type=jnp.float32)
-    up_act = jnp.dot(normed_input, w_mlp_up, preferred_element_type=jnp.float32)
-    mlp_hidden = (jax.nn.silu(gate_act) * up_act).astype(jnp.bfloat16)
-    mlp_term = jnp.dot(mlp_hidden, w_mlp_down, preferred_element_type=jnp.float32)
+    low_rank_part = jnp.dot(
+        conv_out.astype(jnp.bfloat16), w_state_proj, preferred_element_type=jnp.float32
+    )
     own_seqs = cached_inputs.shape[0]
     window_size = cached_inputs.shape[1]
     seq_start = lax.axis_index("seq") * own_seqs
@@ -154,18 +403,33 @@
         (joint_sum / joint_total[..., None])
         .reshape(own_seqs, heads_here * HEAD_SIZE)
         .astype(jnp.bfloat16)
-    )
-    attended = lax.all_gather(attended_own, "seq", axis=0, tiled=True)
-    attn_cols = jnp.dot(attended, w_attn_out, preferred_element_type=jnp.float32)
+        .astype(jnp.float32)
+    )
+    low_rank, attended = sum_gather(devices, seq_size, low_rank_part, attended_own)
+    step_low = low_rank[:, :rank_size].astype(jnp.bfloat16)
+    input_map = low_rank[:, rank_size : rank_size + state_size]
+    output_map = low_rank[:, rank_size + state_size :]
+    step_size = jax.nn.softplus(
+        jnp.dot(step_low, w_step, preferred_element_type=jnp.float32) + step_bias
+    )
+    decay_rate = jnp.exp(log_decay)
+    state_out = (
+        jnp.exp(-step_size[:, None, :] * decay_rate[None]) * ssm_state
+        + step_size[:, None, :] * input_map[:, :, None] * conv_out[:, None, :]
+    )
+    ssm_mixed = jnp.sum(state_out * output_map[:, :, None], axis=1) + skip_gain * conv_out
+    ssm_gated = (ssm_mixed * jax.nn.silu(gate_input)).astype(jnp.bfloat16)
+    ssm_term = jnp.dot(ssm_gated, w_ssm_out, preferred_element_type=jnp.float32)
+    gate_act = jnp.dot(normed_input, w_mlp_gate, preferred_element_type=jnp.float32)
+    up_act = jnp.dot(normed_input, w_mlp_up, preferred_element_type=jnp.float32)
+    mlp_hidden = (jax.nn.silu(gate_act) * up_act).astype(jnp.bfloat16)
+    mlp_term = jnp.dot(mlp_hidden, w_mlp_down, preferred_element_type=jnp.float32)
+    attn_cols = jnp.dot(attended.astype(jnp.bfloat16), w_attn_out, preferred_element_type=jnp.float32)
     col_start = lax.axis_index("seq") * w_attn_out.shape[1]
     attn_term = lax.dynamic_update_slice(
         jnp.zeros((batch_rows, model_width), jnp.float32), attn_cols, (jnp.int32(0), col_start)
     )
-    other_terms = mlp_term + attn_term
-    summed = ssm_summed + lax.psum_scatter(
-        other_terms, ("grp", "seq"), scatter_dimension=1, tiled=True
-    )
-    hidden_out = (hidden_f + summed).astype(jnp.bfloat16)
+    hidden_out = scatter_sum(devices, seq_size, ssm_term + mlp_term + attn_term, hidden_in)
     return (hidden_out, state_out)
 
 
@@ -196,7 +460,7 @@
         P(),
     )
     return jax.shard_map(
-        per_device,
+        functools.partial(per_device, mesh.size, mesh.shape["seq"]),
         mesh=mesh,
         in_specs=placed,
         out_specs=(P(None, ("grp", "seq")), P(None, None, ("grp", "seq"))),

time: 290 us -> 94.8 us (0.33)
  waiting for transfers between devices: 137 us -> 0 us
  blocking collectives: 89.5 us -> 0 us
  Pallas kernels: 0 us -> 41 us
  between operations: 14.3 us -> 0.91 us
  local copies, waits for them, and re-layouts: 6.37 us -> 12.1 us
    reduce_scatter x1 -> x0, waiting for transfers between devices: 137 us -> none  [per_device(): lax.psum_scatter(ssm_term, ('grp', 'seq'), scatter_dimension=1, tiled=True)]
    all_gather x2 -> x0, blocking collectives: 51.2 us -> none  [the longest x1 44.2 us: per_device(): lax.all_gather(hidden_in, ('grp', 'seq'), axis=1, tiled=True)]
    pallas_call x0 -> x3, Pallas kernels: none -> 41 us  [the longest x1 17.5 us: sum_gather(): pl.pallas_call(functools.partial(sum_gather_kernel, devices, seq_size), o...]
    psum x1 -> x0, blocking collectives: 38.3 us -> none  [per_device(): lax.psum(jnp.dot(conv_out.astype(jnp.bfloat16), w_state_proj, preferred_e...]
  transfers between devices with their start and end apart: 1 -> 0, of which waited for: 1 -> 0; matrix products, arithmetic and copies ran while one was open for 0% -> 0% of each run, Pallas kernels for 0% -> 0%
where the time goes in v1:
time: 94.8 us; the launch traced here: 94.1 us
  Pallas kernels  41 us (43%)
  matrix products  37 us (39%)
  local copies, waits for them, and re-layouts  12.1 us (13%)
  other arithmetic  3.15 us (3%)
    pallas_call x1, Pallas kernels, sum_gather(): pl.pallas_call(functools.partial(sum_gather_kernel, devices, seq_size), o...  17.5 us
    pallas_call x1, Pallas kernels, norm_gather(): pl.pallas_call(functools.partial(norm_gather_kernel, devices, seq_size),...  13.1 us
    pallas_call x1, Pallas kernels, scatter_sum(): pl.pallas_call(functools.partial(scatter_sum_kernel, devices, seq_size),...  10.4 us
    dot_general x1, matrix products, per_device(): jnp.dot(flat_inputs, value_projection, preferred_element_type=jnp.float32)  7.38 us
    dot_general x1, matrix products, per_device(): jnp.dot(flat_inputs, key_projection, preferred_element_type=jnp.float32)  7.13 us
    dot_general x1, matrix products, per_device(): jnp.dot(mlp_hidden, w_mlp_down, preferred_element_type=jnp.float32)  5.08 us
    dot_general x1, local copies, waits for them, and re-layouts, per_device(): jnp.dot(flat_inputs, key_projection, preferred_element_type=jnp.float32)  4.15 us
    dot_general x1, matrix products, per_device(): ssm_term = jnp.dot(ssm_gated, w_ssm_out, preferred_element_type=jnp.float32)  3.51 us

profile of v1, /device:TPU:0, one launch (start us, length us, event | category | flops | bytes accessed | tf_op | source)
XLA Modules:
  0.0 94.1 jit_solution(10612193576282012658)
XLA Ops:
  0.7 13.1 %shard_map.230 = bf16[24,4096]{1,0:T(8,128)(2,1)} custom-call(bf16[24,128]{1,0:T(8,128)(2,1)} %hidden_ref.1, f32[1,4096]{1,0:T(1,128)} %bitcast.40), custom_call_target="tpu_custom_call" | custom-call | tf_op jit(solution)/shard_map/pallas_call | solution.py:102
  13.8 2.9 %fusion.23 = f32[3,512]{1,0:T(4,128)S(1)} fusion(bf16[4096,512]{1,0:T(8,128)(2,1)} %param.37, bf16[24,4096]{1,0:T(8,128)(2,1)} %shard_map.230, s32[]{:T(128)S(6)} %select_n.18), kind=kOutput, calls=%fused_computation.44 | convolution fusion | flops 12582912 | bytes 4233220 | tf_op jit(solution)/shard_map/dot_general | solution.py:356
  16.8 0.1 multiply_cosine_fusion.1
  17.1 0.5 multiply_cosine_fusion
  17.6 4.1 %copy.32 = bf16[256,4096]{1,0:T(8,128)(2,1)} copy(bf16[256,4096]{0,1:T(8,128)(2,1)} %bitcast.38) | data formatting | bytes 4194304 | tf_op jit(solution)/shard_map/dot_general | solution.py:375
  21.8 7.1 %fusion = f32[3,512,2,128]{1,3,2,0:T(8,128)S(1)} fusion(bf16[2,128,4096,1]{2,1,0,3:T(8,128)(2,1)} %bitcast.39, bf16[3,512,4096]{2,1,0:T(8,128)(2,1)} %param.44), kind=kOutput, calls=%fused_computation | convolution fusion | flops 3221225472 | bytes 16252928 | tf_op jit(solution)/shard_map/dot_general | solution.py:375
  28.9 0.3 subtract_convert_fusion
  29.3 0.3 fusion.43
  29.6 0.9 copy-done.1
  30.5 0.4 fusion.21
  31.1 0.2 fusion.31
  31.3 0.2 fusion.30
  31.5 0.6 fusion.40
  32.1 0.4 fusion.8
  32.5 0.6 reshape.153
  33.1 7.4 %convolution_convert_fusion = bf16[1536,256]{1,0:T(8,128)(2,1)} fusion(bf16[1536,4096]{1,0:T(8,128)(2,1)} %bitcast.49, bf16[4096,256]{1,0:T(8,128)(2,1)S(1)} %copy-done), kind=kOutput, calls=%fused_computation.3 | convolution fusion | flops 3221618688 | bytes 15466496 | tf_op jit(solution)/shard_map/dot_general | solution.py:380
  40.4 2.0 %reshape.152 = bf16[3,512,2,128]{3,2,1,0:T(2,128)(2,1)S(1)} reshape(bf16[1536,256]{1,0:T(8,128)(2,1)} %convolution_convert_fusion) | data formatting | bytes 1572864 | tf_op jit(solution)/shard_map/reshape | solution.py:382
  42.5 1.6 %fusion.7 = f32[3,2,2,128]{3,2,1,0:T(2,128)} fusion(bf16[3,512,2,128]{3,2,1,0:T(2,128)(2,1)S(1)} %reshape.152, f32[3,2,2,512]{3,2,1,0:T(2,128)S(1)} %get-tuple-element.25, pred[3,512]{1,0:T(4,128)(4,1)} %copy-done.10, f32[3,2,2]{2,1,0:T(2,128)S(1)} %multiply_maximum_fusion, f32[3,2,2]{2,1,0:T(2,128)} %get-tuple-element.8, f32[3,2,128]{2,1,0:T(2,128)} %reshape.153, ...), kind=kOutput, calls=%fused_computation.15 | convolution fusion | flops 1592832 | bytes 821904 | tf_op jit(solution)/shard_map/bkgp,bpkd->bkgd/dot_general | solution.py:399
  44.2 1.4 %reshape.154.att_ref = f32[3,512]{1,0:T(4,128)} reshape(f32[3,2,2,128]{3,2,1,0:T(2,128)} %fusion.7) | data formatting | bytes 12288 | tf_op jit(solution)/shard_map/convert_element_type | solution.py:406
  45.6 2.0 %convolution_convert_fusion.1 = bf16[24,256]{1,0:T(8,128)(2,1)S(1)} fusion(bf16[24,4096]{1,0:T(8,128)(2,1)S(1)} %copy-done.2, bf16[4096,256]{1,0:T(8,128)(2,1)} %param.25), kind=kOutput, calls=%fused_computation.11 | convolution fusion | flops 50337792 | bytes 2306048 | tf_op jit(solution)/shard_map/dot_general | solution.py:329
  47.6 0.8 fusion.27.part_ref
  48.4 17.5 %shard_map.231 = (f32[24,288]{1,0:T(8,128)}, f32[24,512]{1,0:T(8,128)}) custom-call(f32[24,288]{1,0:T(8,128)} %fusion.27.part_ref, f32[3,512]{1,0:T(4,128)} %reshape.154.att_ref), custom_call_target="tpu_custom_call" | custom-call | tf_op jit(solution)/shard_map/pallas_call | solution.py:229
  66.0 0.9 fusion.44
  66.9 0.9 fusion.42
  67.8 0.9 multiply_reduce_fusion
  68.7 3.5 %fusion.25 = f32[24,4096]{1,0:T(8,128)S(1)} fusion(bf16[256,4096]{1,0:T(8,128)(2,1)} %param.36, f32[24,256]{1,0:T(8,128)S(1)} %get-tuple-element.6, f32[24,256]{1,0:T(8,128)S(1)} %divide_multiply_fusion, f32[256]{0:T(256)S(1)} %copy-done.14, bf16[24,4096]{1,0:T(8,128)(2,1)S(1)} %copy-done.2, bf16[4096,256]{1,0:T(8,128)(2,1)} %param.26), kind=kOutput, calls=%fused_computation.46 | convolution fusion | flops 100712448 | bytes 4834304 | tf_op jit(solution)/shard_map/dot_general | solution.py:422
  72.2 3.1 %fusion.47 = f32[24,448]{1,0:T(8,128)S(1)} fusion(bf16[24,4096]{1,0:T(8,128)(2,1)S(1)} %copy-done.2, bf16[4096,448]{0,1:T(8,128)(2,1)} %param.41), kind=kOutput, calls=%fused_computation.80 | convolution fusion | flops 88080384 | bytes 3909632 | tf_op jit(solution)/shard_map/dot_general | solution.py:423
  75.3 5.1 %convolution_add_fusion = f32[24,4096]{1,0:T(8,128)S(1)} fusion(f32[24,4096]{1,0:T(8,128)S(1)} %fusion.25, bf16[448,4096]{1,0:T(8,128)(2,1)} %param.43, bf16[24,4096]{1,0:T(8,128)(2,1)S(1)} %copy-done.2, bf16[4096,448]{0,1:T(8,128)(2,1)} %param.42, f32[24,448]{1,0:T(8,128)S(1)} %fusion.47), kind=kOutput, calls=%fused_computation.2 | convolution fusion | flops 176323584 | bytes 8366080 | tf_op jit(solution)/shard_map/dot_general | solution.py:426
  80.4 1.2 %fusion.2.term_ref = f32[24,4096]{1,0:T(8,128)S(1)} fusion(f32[24,4096]{1,0:T(8,128)S(1)} %convolution_add_fusion, s32[]{:T(128)S(6)} %select_n.22, bf16[512,512]{1,0:T(8,128)(2,1)} %param.40, f32[24,512]{1,0:T(8,128)S(1)} %copy-done.7), kind=kOutput, calls=%fused_computation.6 | convolution fusion | flops 12607488 | bytes 671748 | tf_op jit(solution)/shard_map/dot_general | solution.py:427
  81.7 0.8 copy-done.3
  82.4 10.4 %shard_map.232 = bf16[24,128]{1,0:T(8,128)(2,1)} custom-call(f32[24,4096]{1,0:T(8,128)} %copy-done.3, bf16[24,128]{1,0:T(8,128)(2,1)} %hidden_ref.1), custom_call_target="tpu_custom_call" | custom-call | tf_op jit(solution)/shard_map/pallas_call | solution.py:284
  92.8 1.3 %copy.39 = bf16[24,128]{1,0:T(8,128)(2,1)} copy(bf16[24,128]{1,0:T(8,128)(2,1)} %shard_map.232) | data formatting | bytes 12288
  (44 shorter events, 0.6 us)
Async XLA Ops:
  0.6 31.5 %copy-start = (bf16[4096,256]{1,0:T(8,128)(2,1)S(1)}, bf16[4096,256]{1,0:T(8,128)(2,1)}, u32[]{:S(2)}) copy-start(bf16[4096,256]{1,0:T(8,128)(2,1)} %param.39) | copy-start | bytes 6291460
  13.8 2.9 %copy-start.15 = (s32[24]{0:T(128)S(1)}, s32[24]{0:T(128)}, u32[]{:S(2)}) copy-start(s32[24]{0:T(128)} %param.45) | copy-start | bytes 292
  17.1 14.2 %copy-start.10 = (pred[3,512]{1,0:T(4,128)(4,1)}, pred[3,512]{1,0:T(4,128)(4,1)S(1)}, u32[]{:S(2)}) copy-start(pred[3,512]{1,0:T(4,128)(4,1)S(1)} %iota_compare_fusion) | copy-start | bytes 4612
  28.9 1.6 %copy-start.1 = (bf16[4096,256]{1,0:T(8,128)(2,1)S(1)}, bf16[4096,256]{1,0:T(8,128)(2,1)}, u32[]{:S(2)}) copy-start(bf16[4096,256]{1,0:T(8,128)(2,1)} %param.38) | copy-start | bytes 6291460
  28.9 1.6 %copy-start.2 = (bf16[24,4096]{1,0:T(8,128)(2,1)S(1)}, bf16[24,4096]{1,0:T(8,128)(2,1)}, u32[]{:S(2)}) copy-start(bf16[24,4096]{1,0:T(8,128)(2,1)} %shard_map.230) | copy-start | bytes 589828
  42.5 5.1 %copy-start.8 = (bf16[24,3,256]{2,0,1:T(8,128)(2,1)S(1)}, bf16[24,3,256]{2,0,1:T(8,128)(2,1)}, u32[]{:S(2)}) copy-start(bf16[24,3,256]{2,0,1:T(8,128)(2,1)} %param.29) | copy-start | bytes 110596
  42.5 25.3 %copy-start.9 = (f32[16,256]{1,0:T(8,128)S(1)}, f32[16,256]{1,0:T(8,128)}, u32[]{:S(2)}) copy-start(f32[16,256]{1,0:T(8,128)} %param.33) | copy-start | bytes 49156
  42.5 25.3 %copy-start.4 = (f32[24,16,256]{2,1,0:T(8,128)S(1)}, f32[24,16,256]{2,1,0:T(8,128)}, u32[]{:S(2)}) copy-start(f32[24,16,256]{2,1,0:T(8,128)} %param.35) | copy-start | bytes 1179652
  44.1 3.4 %copy-start.11 = (f32[4,256]{1,0:T(4,128)S(1)}, f32[4,256]{1,0:T(4,128)}, u32[]{:S(2)}) copy-start(f32[4,256]{1,0:T(4,128)} %param.27) | copy-start | bytes 12292
  44.1 3.5 %copy-start.12 = (f32[256]{0:T(256)S(1)}, f32[256]{0:T(256)}, u32[]{:S(2)}) copy-start(f32[256]{0:T(256)} %param.28) | copy-start | bytes 3076
  44.1 3.5 %copy-start.5 = (bf16[256,288]{0,1:T(8,128)(2,1)S(1)}, bf16[256,288]{0,1:T(8,128)(2,1)}, u32[]{:S(2)}) copy-start(bf16[256,288]{0,1:T(8,128)(2,1)} %param.30) | copy-start | bytes 442372
  44.1 21.8 %copy-start.6 = (bf16[256,256]{1,0:T(8,128)(2,1)S(1)}, bf16[256,256]{1,0:T(8,128)(2,1)}, u32[]{:S(2)}) copy-start(bf16[256,256]{1,0:T(8,128)(2,1)} %param.31) | copy-start | bytes 393220
  44.2 21.8 %copy-start.13 = (f32[256]{0:T(256)S(1)}, f32[256]{0:T(256)}, u32[]{:S(2)}) copy-start(f32[256]{0:T(256)} %param.32) | copy-start | bytes 3076
  44.2 24.5 %copy-start.14 = (f32[256]{0:T(256)S(1)}, f32[256]{0:T(256)}, u32[]{:S(2)}) copy-start(f32[256]{0:T(256)} %param.34) | copy-start | bytes 3076
  75.3 5.1 %copy-start.7 = (f32[24,512]{1,0:T(8,128)S(1)}, f32[24,512]{1,0:T(8,128)}, u32[]{:S(2)}) copy-start(f32[24,512]{1,0:T(8,128)} %get-tuple-element.5) | copy-start | bytes 147460
  81.7 0.8 copy-start.3

commit v2 on v1

--- a/solution.py
+++ b/solution.py
@@ -16,73 +16,57 @@
 rope_base = 10000.0
 
 
-def apply_rotary(head_values, positions):
-    half_dim = head_values.shape[-1] // 2
-    frequency = rope_base ** (
-        -(jnp.arange(half_dim, dtype=jnp.float32) * 2.0) / head_values.shape[-1]
-    )
-    angles = positions[..., None, None] * frequency
-    cosine = jnp.cos(angles)
-    sine_part = jnp.sin(angles)
-    front_half = head_values[..., :half_dim]
-    back_half = head_values[..., half_dim:]
-    return jnp.concatenate(
-        [front_half * cosine - back_half * sine_part, back_half * cosine + front_half * sine_part],
-        axis=-1,
-    )
-
-
 def my_index(seq_size):
     return lax.axis_index("grp") * seq_size + lax.axis_index("seq")
 
 
-def device_at(index, seq_size):
-    return (index // seq_size, index % seq_size)
+def each_peer(groups, seq_size, action):
+    group = lax.axis_index("grp")
+    place = lax.axis_index("seq")
+    group_at = [lax.rem(group + dg, groups) for dg in range(groups)]
+
+    def step(ds, carry):
+        there = lax.rem(place + ds, seq_size)
+        for dg in range(groups):
+            action(dg * seq_size + ds, (group_at[dg], there))
+        return carry
+
+    for dg in range(1, groups):
+        action(dg * seq_size, (group_at[dg], place))
+    lax.fori_loop(1, seq_size, step, 0)
 
 
 def meet_all(devices, seq_size):
-    me = my_index(seq_size)
     barrier = pltpu.get_barrier_semaphore()
-
-    def greet(k, carry):
-        pl.semaphore_signal(
-            barrier,
-            inc=1,
-            device_id=device_at(lax.rem(me + k, devices), seq_size),
-            device_id_type=MESH,
-        )
-        return carry
-
-    lax.fori_loop(1, devices, greet, 0)
+    each_peer(
+        devices // seq_size,
+        seq_size,
+        lambda k, where: pl.semaphore_signal(
+            barrier, inc=1, device_id=where, device_id_type=MESH
+        ),
+    )
     pl.semaphore_wait(barrier, devices - 1)
-
-
-def each_peer(devices, action):
-    def step(k, carry):
-        action(k)
-        return carry
-
-    lax.fori_loop(1, devices, step, 0)
 
 
 def norm_gather_kernel(devices, seq_size, x_ref, gain_ref, out_ref, buf, send_sem, recv_sem):
     me = my_index(seq_size)
+    groups = devices // seq_size
     width = x_ref.shape[1]
     meet_all(devices, seq_size)
 
-    def copy_for(k):
+    def copy_for(k, where):
         return pltpu.make_async_remote_copy(
             src_ref=x_ref,
             dst_ref=buf.at[me],
             send_sem=send_sem.at[k],
             recv_sem=recv_sem.at[k],
-            device_id=device_at(lax.rem(me + k, devices), seq_size),
+            device_id=where,
             device_id_type=MESH,
         )
 
-    each_peer(devices, lambda k: copy_for(k).start())
+    each_peer(groups, seq_size, lambda k, where: copy_for(k, where).start())
     buf[me] = x_ref[...]
-    each_peer(devices, lambda k: copy_for(k).wait())
+    each_peer(groups, seq_size, lambda k, where: copy_for(k, where).wait())
     total = jnp.zeros(x_ref.shape, jnp.float32)
     for d in range(devices):
         block = buf[d].astype(jnp.float32)
@@ -109,7 +93,12 @@
             pltpu.SemaphoreType.DMA((devices,)),
             pltpu.SemaphoreType.DMA((devices,)),
         ],
-        compiler_params=pltpu.CompilerParams(collective_id=0, has_side_effects=True),
+        compiler_params=pltpu.CompilerParams(
+            collective_id=0, has_side_effects=True, vmem_limit_bytes=8 * 1024 * 1024
+        ),
+        cost_estimate=pl.CostEstimate(
+            flops=2_000_000_000, bytes_accessed=30_000_000, transcendentals=0
+        ),
     )(hidden_in, norm_gain.reshape(1, -1))
 
 
@@ -133,6 +122,7 @@
     att_recv_sem,
 ):
     me = my_index(seq_size)
+    groups = devices // seq_size
     group = lax.axis_index("grp")
     place = lax.axis_index("seq")
     owners, each = split.shape[0], split.shape[1]
@@ -141,26 +131,36 @@
         split[r] = part_ref[r * each : (r + 1) * each, :]
     meet_all(devices, seq_size)
 
-    def peer(k):
-        return lax.rem(me + k, devices)
-
-    def part_copy(k):
+    def index_of(where):
+        return where[0] * seq_size + where[1]
+
+    def part_copy(k, where):
         return pltpu.make_async_remote_copy(
-            src_ref=split.at[lax.rem(peer(k), owners)],
+            src_ref=split.at[index_of(where)],
             dst_ref=landed.at[me],
             send_sem=send_sem.at[k],
             recv_sem=recv_sem.at[k],
-            device_id=device_at(peer(k), seq_size),
+            device_id=where,
             device_id_type=MESH,
         )
 
-    def full_copy(k):
+    def land_copy(k, where):
         return pltpu.make_async_remote_copy(
             src_ref=reduced,
-            dst_ref=full.at[lax.rem(me, owners)],
+            dst_ref=landed.at[me],
+            send_sem=send_sem.at[k],
+            recv_sem=recv_sem.at[k],
+            device_id=where,
+            device_id_type=MESH,
+        )
+
+    def full_copy(k, where):
+        return pltpu.make_async_remote_copy(
+            src_ref=reduced,
+            dst_ref=full.at[me],
             send_sem=send_all_sem.at[k],
             recv_sem=recv_all_sem.at[k],
-            device_id=device_at(peer(k), seq_size),
+            device_id=where,
             device_id_type=MESH,
         )
 
@@ -174,46 +174,67 @@
             device_id_type=MESH,
         )
 
-    def start_part(k):
-        @pl.when(peer(k) < owners)
+    def each_place(action):
+        def step(k, carry):
+            action(k)
+            return carry
+
+        lax.fori_loop(1, seq_size, step, 0)
+
+    def start_part(k, where):
+        @pl.when(index_of(where) < owners)
         def _():
-            part_copy(k).start()
-
-    each_peer(devices, start_part)
-    each_peer(seq_size, lambda k: att_copy(k).start())
+            part_copy(k, where).start()
+
+    each_peer(groups, seq_size, start_part)
+    each_place(lambda k: att_copy(k).start())
     att_buf[place] = att_ref[...]
 
     @pl.when(me < owners)
     def _():
         landed[me] = split[me]
-        each_peer(devices, lambda k: part_copy(k).wait_recv())
+        each_peer(groups, seq_size, lambda k, where: land_copy(k, where).wait_recv())
         total = landed[0]
         for d in range(1, devices):
             total = total + landed[d]
         reduced[...] = total
         full[me] = total
-        each_peer(devices, lambda k: full_copy(k).start())
-
-    def end_part(k):
-        @pl.when(peer(k) < owners)
+        each_peer(groups, seq_size, lambda k, where: full_copy(k, where).start())
+
+    def end_part(k, where):
+        @pl.when(index_of(where) < owners)
         def _():
-            part_copy(k).wait_send()
-
-    each_peer(devices, end_part)
-    each_peer(seq_size, lambda k: att_copy(k).wait())
+            part_copy(k, where).wait_send()
+
+    each_peer(groups, seq_size, end_part)
+    each_place(lambda k: att_copy(k).wait())
     for s in range(seq_size):
         att_out_ref[s * own_rows : (s + 1) * own_rows, :] = att_buf[s]
 
-    def end_full(k):
-        @pl.when(lax.rem(me + devices - k, devices) < owners)
-        def _():
-            full_copy(k).wait_recv()
-
-    each_peer(devices, end_full)
+    def end_full(ds, carry):
+        there = lax.rem(place + seq_size - ds, seq_size)
+        for dg in range(groups):
+            source = lax.rem(group + groups - dg, groups) * seq_size + there
+            k = dg * seq_size + ds
+
+            @pl.when(jnp.logical_and(source < owners, k > 0))
+            def _():
+                pltpu.make_async_remote_copy(
+                    src_ref=reduced,
+                    dst_ref=full.at[source],
+                    send_sem=send_all_sem.at[k],
+                    recv_sem=recv_all_sem.at[k],
+                    device_id=(group, lax.rem(place + 1, seq_size)),
+                    device_id_type=MESH,
+                ).wait_recv()
+
+        return carry
+
+    lax.fori_loop(0, seq_size, end_full, 0)
 
     @pl.when(me < owners)
     def _():
-        each_peer(devices, lambda k: full_copy(k).wait_send())
+        each_peer(groups, seq_size, lambda k, where: full_copy(k, where).wait_send())
 
     for r in range(owners):
         out_ref[r * each : (r + 1) * each, :] = full[r]
@@ -247,7 +268,12 @@
             dma((seq_size,)),
             dma((seq_size,)),
         ],
-        compiler_params=pltpu.CompilerParams(collective_id=1, has_side_effects=True),
+        compiler_params=pltpu.CompilerParams(
+            collective_id=1, has_side_effects=True, vmem_limit_bytes=8 * 1024 * 1024
+        ),
+        cost_estimate=pl.CostEstimate(
+            flops=2_000_000_000, bytes_accessed=30_000_000, transcendentals=0
+        ),
     )(part, att)
 
 
@@ -255,24 +281,25 @@
     devices, seq_size, term_ref, hidden_ref, out_ref, outgoing, landed, send_sem, recv_sem
 ):
     me = my_index(seq_size)
+    groups = devices // seq_size
     width = hidden_ref.shape[1]
     for d in range(devices):
         outgoing[d] = term_ref[:, d * width : (d + 1) * width].astype(jnp.bfloat16)
     meet_all(devices, seq_size)
 
-    def copy_for(k):
+    def copy_for(k, where):
         return pltpu.make_async_remote_copy(
-            src_ref=outgoing.at[lax.rem(me + k, devices)],
+            src_ref=outgoing.at[where[0] * seq_size + where[1]],
             dst_ref=landed.at[me],
             send_sem=send_sem.at[k],
             recv_sem=recv_sem.at[k],
-            device_id=device_at(lax.rem(me + k, devices), seq_size),
+            device_id=where,
             device_id_type=MESH,
         )
 
-    each_peer(devices, lambda k: copy_for(k).start())
+    each_peer(groups, seq_size, lambda k, where: copy_for(k, where).start())
     landed[me] = outgoing[me]
-    each_peer(devices, lambda k: copy_for(k).wait())
+    each_peer(groups, seq_size, lambda k, where: copy_for(k, where).wait())
     total = landed[0].astype(jnp.float32)
     for d in range(1, devices):
         total = total + landed[d].astype(jnp.float32)
@@ -292,8 +319,165 @@
             pltpu.SemaphoreType.DMA((devices,)),
             pltpu.SemaphoreType.DMA((devices,)),
         ],
-        compiler_params=pltpu.CompilerParams(collective_id=2, has_side_effects=True),
+        compiler_params=pltpu.CompilerParams(
+            collective_id=2, has_side_effects=True, vmem_limit_bytes=8 * 1024 * 1024
+        ),
+        cost_estimate=pl.CostEstimate(
+            flops=2_000_000_000, bytes_accessed=30_000_000, transcendentals=0
+        ),
     )(term, hidden_in)
+
+
+def window_kernel(
+    own,
+    kv_here,
+    heads_per_group,
+    normed_ref,
+    cos_ref,
+    sin_ref,
+    cos_new_ref,
+    sin_new_ref,
+    bias_ref,
+    cached_ref,
+    wk_ref,
+    wv_ref,
+    wq_ref,
+    out_ref,
+    x_buf,
+    wkv,
+    wq,
+    k_buf,
+    v_buf,
+    new_rows,
+    x_sem,
+    w_sem,
+):
+    tiles, tile = x_buf.shape[0], x_buf.shape[1]
+    per_seq = tiles // own
+    window = per_seq * tile
+    kv_width = kv_here * HEAD_SIZE
+    q_width = wq.shape[1]
+    copy_k = pltpu.make_async_copy(wk_ref, wkv.at[:, pl.ds(0, kv_width)], w_sem.at[0])
+    copy_v = pltpu.make_async_copy(wv_ref, wkv.at[:, pl.ds(kv_width, kv_width)], w_sem.at[1])
+    copy_q = pltpu.make_async_copy(wq_ref, wq, w_sem.at[2])
+    copy_k.start()
+    copy_v.start()
+    for t in range(tiles):
+        pltpu.make_async_copy(cached_ref.at[t], x_buf.at[t], x_sem.at[t]).start()
+    copy_q.start()
+    copy_k.wait()
+    copy_v.wait()
+
+    def turned(values, cosine, sine):
+        return (values * cosine + pltpu.roll(values, HEAD_SIZE // 2, 1) * sine).astype(
+            jnp.bfloat16
+        )
+
+    def project(t, carry):
+        pltpu.make_async_copy(cached_ref.at[t], x_buf.at[t], x_sem.at[t]).wait()
+        rows = jnp.dot(x_buf[t], wkv[...], preferred_element_type=jnp.float32)
+        slots = pl.ds(pl.multiple_of(lax.rem(t, per_seq) * tile, tile), tile)
+        cosine, sine = cos_ref[slots, :], sin_ref[slots, :]
+        here = pl.ds(pl.multiple_of(t * tile, tile), tile)
+        for h in range(kv_here):
+            cols = slice(h * HEAD_SIZE, (h + 1) * HEAD_SIZE)
+            k_buf[here, cols] = turned(rows[:, cols], cosine, sine)
+        v_buf[here, :] = rows[:, kv_width:].astype(jnp.bfloat16)
+        return carry
+
+    lax.fori_loop(0, tiles, project, 0)
+    copy_q.wait()
+    normed = normed_ref[...]
+    new_rows[:, :q_width] = jnp.dot(normed, wq[...], preferred_element_type=jnp.float32)
+    new_rows[:, q_width:] = jnp.dot(normed, wkv[...], preferred_element_type=jnp.float32)
+    first = lax.axis_index("seq") * own
+    scale = HEAD_SIZE ** (-0.5)
+    for b in range(own):
+        row = new_rows[pl.ds(first + b, 1), :]
+        cosine, sine = cos_new_ref[b : b + 1, :], sin_new_ref[b : b + 1, :]
+        here = slice(b * window, (b + 1) * window)
+        for h in range(kv_here):
+            cols = slice(h * HEAD_SIZE, (h + 1) * HEAD_SIZE)
+            heads = range(h * heads_per_group, (h + 1) * heads_per_group)
+            query = turned(
+                jnp.concatenate(
+                    [row[:, q * HEAD_SIZE : (q + 1) * HEAD_SIZE] for q in heads], axis=0
+                ),
+                cosine,
+                sine,
+            )
+            at = q_width + h * HEAD_SIZE
+            fresh_key = turned(row[:, at : at + HEAD_SIZE], cosine, sine)
+            at += kv_width
+            fresh_value = row[:, at : at + HEAD_SIZE].astype(jnp.bfloat16).astype(jnp.float32)
+            scores = lax.dot_general(
+                query,
+                k_buf[here, cols],
+                (((1,), (1,)), ((), ())),
+                preferred_element_type=jnp.float32,
+            )
+            scores = scores * scale + bias_ref[b : b + 1, :]
+            fresh = (
+                jnp.sum(
+                    query.astype(jnp.float32) * fresh_key.astype(jnp.float32),
+                    axis=1,
+                    keepdims=True,
+                )
+                * scale
+            )
+            top = jnp.maximum(jnp.max(scores, axis=1, keepdims=True), fresh)
+            weights = jnp.exp(scores - top)
+            weight_new = jnp.exp(fresh - top)
+            total = jnp.sum(weights, axis=1, keepdims=True) + weight_new
+            mixed = jnp.dot(
+                weights.astype(jnp.bfloat16), v_buf[here, cols], preferred_element_type=jnp.float32
+            )
+            mixed = (mixed + weight_new * fresh_value) / total
+            mixed = mixed.astype(jnp.bfloat16).astype(jnp.float32)
+            for i, q in enumerate(heads):
+                out_ref[b : b + 1, q * HEAD_SIZE : (q + 1) * HEAD_SIZE] = mixed[i : i + 1, :]
+
+
+def rotary_tables(positions):
+    half_dim = HEAD_SIZE // 2
+    frequency = rope_base ** (-(jnp.arange(half_dim, dtype=jnp.float32) * 2.0) / HEAD_SIZE)
+    angles = positions[:, None] * frequency
+    cosine, sine = jnp.cos(angles), jnp.sin(angles)
+    return (
+        jnp.concatenate([cosine, cosine], axis=1),
+        jnp.concatenate([-sine, sine], axis=1),
+    )
+
+
+def window_attention(normed, cached, wk, wv, wq, lengths):
+    own, window, width = cached.shape
+    tile = 256 if window % 256 == 0 else window
+    tiles = own * window // tile
+    kv_width, q_width = wk.shape[1], wq.shape[1]
+    slots = jnp.arange(window, dtype=jnp.int32)
+    cosine, sine = rotary_tables(slots.astype(jnp.float32))
+    cos_new, sin_new = rotary_tables(lengths.astype(jnp.float32))
+    bias = jnp.where(slots[None, :] < lengths[:, None], 0.0, -1e30).astype(jnp.float32)
+    any_spec = pl.BlockSpec(memory_space=pl.ANY)
+    return pl.pallas_call(
+        functools.partial(
+            window_kernel, own, kv_width // HEAD_SIZE, q_width // kv_width
+        ),
+        out_shape=jax.ShapeDtypeStruct((own, q_width), jnp.float32),
+        in_specs=[VMEM_SPEC] * 6 + [any_spec] * 4,
+        out_specs=VMEM_SPEC,
+        scratch_shapes=[
+            pltpu.VMEM((tiles, tile, width), jnp.bfloat16),
+            pltpu.VMEM((width, 2 * kv_width), jnp.bfloat16),
+            pltpu.VMEM((width, q_width), jnp.bfloat16),
+            pltpu.VMEM((own * window, kv_width), jnp.bfloat16),
+            pltpu.VMEM((own * window, kv_width), jnp.bfloat16),
+            pltpu.VMEM((normed.shape[0], q_width + 2 * kv_width), jnp.float32),
+            pltpu.SemaphoreType.DMA((tiles,)),
+            pltpu.SemaphoreType.DMA((3,)),
+        ],
+        compiler_params=pltpu.CompilerParams(vmem_limit_bytes=48 * 1024 * 1024),
+    )(normed, cosine, sine, cos_new, sin_new, bias, cached.reshape(tiles, tile, width), wk, wv, wq)
 
 
 def per_device(
@@ -343,67 +527,10 @@
         conv_out.astype(jnp.bfloat16), w_state_proj, preferred_element_type=jnp.float32
     )
     own_seqs = cached_inputs.shape[0]
-    window_size = cached_inputs.shape[1]
     seq_start = lax.axis_index("seq") * own_seqs
-    normed_own = lax.dynamic_slice_in_dim(normed_input, seq_start, own_seqs, 0)
     lengths_own = lax.dynamic_slice_in_dim(window_lengths, seq_start, own_seqs, 0)
-    heads_here = w_query.shape[1] // HEAD_SIZE
-    kv_here = key_projection.shape[1] // HEAD_SIZE
-    heads_per_group = heads_here // kv_here
-    attention_scale = HEAD_SIZE ** (-0.5)
-    fresh_position = lengths_own.astype(jnp.float32)
-    query = apply_rotary(
-        jnp.dot(normed_own, w_query, preferred_element_type=jnp.float32).reshape(
-            own_seqs, heads_here, HEAD_SIZE
-        ),
-        fresh_position,
-    ).astype(jnp.bfloat16)
-    fresh_key = apply_rotary(
-        jnp.dot(normed_own, key_projection, preferred_element_type=jnp.float32).reshape(
-            own_seqs, kv_here, HEAD_SIZE
-        ),
-        fresh_position,
-    ).astype(jnp.bfloat16)
-    fresh_value = (
-        jnp.dot(normed_own, value_projection, preferred_element_type=jnp.float32)
-        .astype(jnp.bfloat16)
-        .reshape(own_seqs, kv_here, HEAD_SIZE)
-    )
-    flat_inputs = cached_inputs.reshape(own_seqs * window_size, model_width)
-    slot_ids = jnp.arange(window_size, dtype=jnp.int32)
-    positions = jnp.broadcast_to(slot_ids[None, :], (own_seqs, window_size)).astype(jnp.float32)
-    window_key_rows = jnp.dot(
-        flat_inputs, key_projection, preferred_element_type=jnp.float32
-    ).reshape(own_seqs, window_size, kv_here, HEAD_SIZE)
-    window_key_rows = apply_rotary(window_key_rows, positions).astype(jnp.bfloat16)
-    window_value_rows = (
-        jnp.dot(flat_inputs, value_projection, preferred_element_type=jnp.float32)
-        .astype(jnp.bfloat16)
-        .reshape(own_seqs, window_size, kv_here, HEAD_SIZE)
-    )
-    grouped_query = query.astype(jnp.float32).reshape(own_seqs, kv_here, heads_per_group, HEAD_SIZE)
-    scores = (
-        jnp.einsum("bkgd,bpkd->bkgp", grouped_query, window_key_rows.astype(jnp.float32))
-        * attention_scale
-    )
-    fresh_score = (
-        jnp.einsum("ynow,ynw->yno", grouped_query, fresh_key.astype(jnp.float32)) * attention_scale
-    )
-    is_valid = (slot_ids[None, :] < lengths_own[:, None])[:, None, None, :]
-    scores = jnp.where(is_valid, scores, -1e30)
-    joint_max = jnp.maximum(jnp.max(scores, axis=-1), fresh_score)
-    weights = jnp.where(is_valid, jnp.exp(scores - joint_max[..., None]), 0.0)
-    weight_new = jnp.exp(fresh_score - joint_max)
-    joint_total = jnp.sum(weights, axis=-1) + weight_new
-    joint_sum = (
-        jnp.einsum("bkgp,bpkd->bkgd", weights, window_value_rows.astype(jnp.float32))
-        + weight_new[..., None] * fresh_value.astype(jnp.float32)[:, :, None, :]
-    )
-    attended_own = (
-        (joint_sum / joint_total[..., None])
-        .reshape(own_seqs, heads_here * HEAD_SIZE)
-        .astype(jnp.bfloat16)
-        .astype(jnp.float32)
+    attended_own = window_attention(
+        normed_input, cached_inputs, key_projection, value_projection, w_query, lengths_own
     )
     low_rank, attended = sum_gather(devices, seq_size, low_rank_part, attended_own)
     step_low = low_rank[:, :rank_size].astype(jnp.bfloat16)

time: 94.8 us -> 70 us (0.74)
  matrix products: 37 us -> 13 us
  local copies, waits for them, and re-layouts: 12.1 us -> 2.21 us
  Pallas kernels: 41 us -> 50.2 us
    dot_general x8 -> x0, matrix products: 20.4 us -> none  [the longest x1 7.38 us: per_device(): jnp.dot(flat_inputs, value_projection, preferred_element_type=jnp.float32)]
    pallas_call x0 -> x1, Pallas kernels: none -> 13.3 us  [window_attention(): pl.pallas_call(functools.partial(window_kernel, own, kv_width // HEAD_SIZ...]
    dot_general x1 -> x0, local copies, waits for them, and re-layouts: 4.15 us -> none  [per_device(): jnp.dot(flat_inputs, key_projection, preferred_element_type=jnp.float32)]
    pallas_call x1, Pallas kernels: 17.5 us -> 13.9 us  [sum_gather(): pl.pallas_call(functools.partial(sum_gather_kernel, devices, seq_size), o...]
    reshape x3 -> x0, local copies, waits for them, and re-layouts: 2.05 us -> none  [the longest x1 2.01 us: per_device(): window_value_rows = jnp.dot(flat_inputs, value_projection, preferred_elem...]
    convert_element_type x2 -> x0, local copies, waits for them, and re-layouts: 1.98 us -> none  [the longest x1 1.38 us: per_device(): attended_own = (joint_sum / joint_total[..., None]).reshape(own_seqs, hea...]
    dot_general x1, matrix products: 1.98 us -> 0.39 us  [per_device(): jnp.dot(normed_input, w_ssm_in, preferred_element_type=jnp.float32)]
    neg x0 -> x2, other arithmetic: none -> 1.11 us  [rotary_tables(): -sine]
where the time goes in v2:
time: 70 us; the launch traced here: 69.6 us
  Pallas kernels  50.2 us (72%)
  matrix products  13 us (19%)
  other arithmetic  3.32 us (5%)
  local copies, waits for them, and re-layouts  2.21 us (3%)
  between operations  0.89 us (1%)
    pallas_call x1, Pallas kernels, sum_gather(): pl.pallas_call(functools.partial(sum_gather_kernel, devices, seq_size), o...  13.9 us
    pallas_call x1, Pallas kernels, norm_gather(): pl.pallas_call(functools.partial(norm_gather_kernel, devices, seq_size),...  13.3 us
    pallas_call x1, Pallas kernels, window_attention(): pl.pallas_call(functools.partial(window_kernel, own, kv_width // HEAD_SIZ...  13.3 us
    pallas_call x1, Pallas kernels, scatter_sum(): pl.pallas_call(functools.partial(scatter_sum_kernel, devices, seq_size),...  9.75 us
    dot_general x1, matrix products, per_device(): jnp.dot(mlp_hidden, w_mlp_down, preferred_element_type=jnp.float32)  5.08 us
    dot_general x1, matrix products, per_device(): jnp.dot(normed_input, w_mlp_gate, preferred_element_type=jnp.float32)  3.12 us
    dot_general x1, matrix products, per_device(): ssm_term = jnp.dot(ssm_gated, w_ssm_out, preferred_element_type=jnp.float32)  2.88 us
    unnamed x33, local copies, waits for them, and re-layouts  2.13 us

profile of v2, /device:TPU:0, one launch (start us, length us, event | category | flops | bytes accessed | tf_op | source)
XLA Modules:
  0.0 69.6 jit_solution(17544884470797511578)
XLA Ops:
  0.6 0.0 copy-start
  0.6 0.9 %fusion.19 = (f32[3]{0:T(128)S(1)}, s32[3]{0:T(128)S(1)}) fusion(s32[24]{0:T(128)} %param.45, s32[]{:T(128)S(6)} %select_n.14), kind=kLoop, calls=%fused_computation.42 | loop fusion | flops 3 | bytes 40 | tf_op jit(solution)/shard_map/convert_element_type | solution.py:459
  1.5 0.1 fusion.18
  1.7 0.1 pad_maximum_fusion.2
  1.7 1.0 %fusion.2 = (f32[512,64]{1,0:T(8,128)S(1)}, f32[512,64]{1,0:T(8,128)S(1)}, f32[512,64]{1,0:T(8,128)S(1)}) fusion(f32[64]{0:T(128)S(1)} %multiply_power_fusion, f32[512]{0:T(512)S(1)} %iota_convert_fusion), kind=kLoop, calls=%fused_computation.13 | loop fusion | flops 65536 | bytes 395520 | tf_op jit(solution)/shard_map/neg | solution.py:448
  2.7 0.2 pad_maximum_fusion
  3.0 0.1 fusion.15.bias_ref
  3.0 0.7 %copy-done.3 = f32[4096]{0:T(1024)S(1)} copy-done((f32[4096]{0:T(1024)S(1)}, f32[4096]{0:T(1024)}, u32[]{:S(2)}) %copy-start.3) | copy-done | bytes 16408
  3.7 0.7 copy-done.4
  4.4 13.3 %shard_map.230.normed_ref = bf16[24,4096]{1,0:T(8,128)(2,1)S(1)} custom-call(bf16[24,128]{1,0:T(8,128)(2,1)S(1)} %copy-done.4, f32[1,4096]{1,0:T(1,128)S(1)} %bitcast.17), custom_call_target="tpu_custom_call" | custom-call | flops 2000000000 | bytes 30000000 | tf_op jit(solution)/shard_map/pallas_call | solution.py:86
  17.8 0.0 copy-start.6
  17.8 0.0 copy-start.10
  17.8 0.0 copy-start.12
  17.8 0.0 copy-start.13
  17.8 0.0 copy-start.8
  17.9 13.3 %shard_map.231.att_ref = f32[3,512]{1,0:T(4,128)S(1)} custom-call(bf16[24,4096]{1,0:T(8,128)(2,1)S(1)} %shard_map.230.normed_ref, f32[512,128]{1,0:T(8,128)S(1)} %get-tuple-element.20.cos_ref, f32[512,128]{1,0:T(8,128)S(1)} %get-tuple-element.21.sin_ref, f32[3,128]{1,0:T(4,128)S(1)} %get-tuple-element.22.cos_new_ref, ...), custom_call_target="tpu_custom_call" | custom-call | tf_op jit(solution)/shard_map/pallas_call | solution.py:462
  31.1 0.4 convolution_convert_fusion
  31.5 0.0 copy-done.12
  31.6 0.2 fusion.12.part_ref
  31.8 0.0 copy-start.11
  31.8 0.0 copy-start.15
  31.8 13.9 %shard_map.232 = (f32[24,288]{1,0:T(8,128)S(1)}, f32[24,512]{1,0:T(8,128)S(1)}) custom-call(f32[24,288]{1,0:T(8,128)S(1)} %fusion.12.part_ref, f32[3,512]{1,0:T(4,128)S(1)} %shard_map.231.att_ref), custom_call_target="tpu_custom_call" | custom-call | flops 2000000000 | bytes 30000000 | tf_op jit(solution)/shard_map/pallas_call | solution.py:250
  45.7 0.2 fusion.21
  45.9 0.1 fusion.20
  46.0 0.9 %multiply_reduce_fusion = (f32[24,256]{1,0:T(8,128)S(1)}, f32[24,16,256]{2,1,0:T(8,128)}) fusion(f32[24,16]{1,0:T(8,128)S(1)} %get-tuple-element.11, f32[24,256]{1,0:T(8,128)S(1)} %divide_multiply_fusion, f32[24,16]{1,0:T(8,128)S(1)} %get-tuple-element.10, f32[24,256]{1,0:T(8,128)S(1)} %get-tuple-element.19, f32[24,16,256]{2,1,0:T(8,128)S(1)} %copy-done.7, ...), kind=kLoop, calls=%fused_computation.7 | loop fusion | flops 681984 | bytes 904192 | tf_op jit(solution)/shard_map/reduce_sum | solution.py:547
  46.9 2.9 %fusion.10 = f32[24,4096]{1,0:T(8,128)S(1)} fusion(bf16[256,4096]{1,0:T(8,128)(2,1)S(1)} %copy-done, f32[24,256]{1,0:T(8,128)S(1)} %get-tuple-element.6, f32[24,256]{1,0:T(8,128)S(1)} %divide_multiply_fusion, f32[256]{0:T(256)S(1)} %copy-done.15, bf16[24,4096]{1,0:T(8,128)(2,1)S(1)} %shard_map.230.normed_ref, bf16[4096,256]{1,0:T(8,128)(2,1)} %param.26), kind=kOutput, calls=%fused_computation.26 | convolution fusion | flops 100712448 | bytes 4834304 | tf_op jit(solution)/shard_map/dot_general | solution.py:549
  49.8 3.1 %fusion.24 = f32[24,448]{1,0:T(8,128)S(1)} fusion(bf16[24,4096]{1,0:T(8,128)(2,1)S(1)} %shard_map.230.normed_ref, bf16[4096,448]{0,1:T(8,128)(2,1)} %param.41), kind=kOutput, calls=%fused_computation.46 | convolution fusion | flops 88080384 | bytes 3909632 | tf_op jit(solution)/shard_map/dot_general | solution.py:550
  52.9 0.0 copy-start.5
  53.0 5.1 %convolution_add_fusion = f32[24,4096]{1,0:T(8,128)S(1)} fusion(f32[24,4096]{1,0:T(8,128)S(1)} %fusion.10, bf16[448,4096]{1,0:T(8,128)(2,1)} %param.43, bf16[24,4096]{1,0:T(8,128)(2,1)S(1)} %shard_map.230.normed_ref, bf16[4096,448]{0,1:T(8,128)(2,1)} %param.42, f32[24,448]{1,0:T(8,128)S(1)} %fusion.24), kind=kOutput, calls=%fused_computation | convolution fusion | flops 176323584 | bytes 8366080 | tf_op jit(solution)/shard_map/dot_general | solution.py:553
  58.0 1.2 %fusion.term_ref = f32[24,4096]{1,0:T(8,128)S(1)} fusion(f32[24,4096]{1,0:T(8,128)S(1)} %convolution_add_fusion, s32[]{:T(128)S(6)} %select_n.17, bf16[512,512]{1,0:T(8,128)(2,1)} %param.40, f32[24,512]{1,0:T(8,128)S(1)} %get-tuple-element.5), kind=kOutput, calls=%fused_computation.3 | convolution fusion | flops 12607488 | bytes 671748 | tf_op jit(solution)/shard_map/dot_general | solution.py:554
  59.3 9.8 %shard_map.233 = bf16[24,128]{1,0:T(8,128)(2,1)S(1)} custom-call(f32[24,4096]{1,0:T(8,128)S(1)} %fusion.term_ref, bf16[24,128]{1,0:T(8,128)(2,1)S(1)} %copy-done.5), custom_call_target="tpu_custom_call" | custom-call | flops 2000000000 | bytes 30000000 | tf_op jit(solution)/shard_map/pallas_call | solution.py:311
  69.0 0.6 copy.27
  (26 shorter events, 0.1 us)
Async XLA Ops:
  0.6 46.3 %copy-start = (bf16[256,4096]{1,0:T(8,128)(2,1)S(1)}, bf16[256,4096]{1,0:T(8,128)(2,1)}, u32[]{:S(2)}) copy-start(bf16[256,4096]{1,0:T(8,128)(2,1)} %param.36) | copy-start | bytes 6291460
  3.0 0.7 %copy-start.3 = (f32[4096]{0:T(1024)S(1)}, f32[4096]{0:T(1024)}, u32[]{:S(2)}) copy-start(f32[4096]{0:T(1024)} %param.24) | copy-start | bytes 49156
  3.7 0.7 copy-start.4
  4.4 13.3 %copy-start.1 = (bf16[4096,256]{1,0:T(8,128)(2,1)S(1)}, bf16[4096,256]{1,0:T(8,128)(2,1)}, u32[]{:S(2)}) copy-start(bf16[4096,256]{1,0:T(8,128)(2,1)} %wk_ref.1) | copy-start | bytes 6291460
  4.4 13.3 %copy-start.2 = (bf16[4096,256]{1,0:T(8,128)(2,1)S(1)}, bf16[4096,256]{1,0:T(8,128)(2,1)}, u32[]{:S(2)}) copy-start(bf16[4096,256]{1,0:T(8,128)(2,1)} %wv_ref.1) | copy-start | bytes 6291460
  17.8 13.3 %copy-start.6 = (bf16[4096,256]{1,0:T(8,128)(2,1)S(1)}, bf16[4096,256]{1,0:T(8,128)(2,1)}, u32[]{:S(2)}) copy-start(bf16[4096,256]{1,0:T(8,128)(2,1)} %param.25) | copy-start | bytes 6291460
  17.8 13.7 %copy-start.10 = (bf16[24,3,256]{2,0,1:T(8,128)(2,1)S(1)}, bf16[24,3,256]{2,0,1:T(8,128)(2,1)}, u32[]{:S(2)}) copy-start(bf16[24,3,256]{2,0,1:T(8,128)(2,1)} %param.29) | copy-start | bytes 110596
  17.8 13.7 %copy-start.12 = (f32[4,256]{1,0:T(4,128)S(1)}, f32[4,256]{1,0:T(4,128)}, u32[]{:S(2)}) copy-start(f32[4,256]{1,0:T(4,128)} %param.27) | copy-start | bytes 12292
  17.8 13.7 %copy-start.13 = (f32[256]{0:T(256)S(1)}, f32[256]{0:T(256)}, u32[]{:S(2)}) copy-start(f32[256]{0:T(256)} %param.28) | copy-start | bytes 3076
  17.8 13.8 %copy-start.8 = (bf16[256,288]{0,1:T(8,128)(2,1)S(1)}, bf16[256,288]{0,1:T(8,128)(2,1)}, u32[]{:S(2)}) copy-start(bf16[256,288]{0,1:T(8,128)(2,1)} %param.30) | copy-start | bytes 442372
  31.8 13.9 %copy-start.9 = (bf16[256,256]{1,0:T(8,128)(2,1)S(1)}, bf16[256,256]{1,0:T(8,128)(2,1)}, u32[]{:S(2)}) copy-start(bf16[256,256]{1,0:T(8,128)(2,1)} %param.31) | copy-start | bytes 393220
  31.8 13.9 %copy-start.14 = (f32[256]{0:T(256)S(1)}, f32[256]{0:T(256)}, u32[]{:S(2)}) copy-start(f32[256]{0:T(256)} %param.32) | copy-start | bytes 3076
  31.8 14.2 %copy-start.11 = (f32[16,256]{1,0:T(8,128)S(1)}, f32[16,256]{1,0:T(8,128)}, u32[]{:S(2)}) copy-start(f32[16,256]{1,0:T(8,128)} %param.33) | copy-start | bytes 49156
  31.8 14.2 %copy-start.7 = (f32[24,16,256]{2,1,0:T(8,128)S(1)}, f32[24,16,256]{2,1,0:T(8,128)}, u32[]{:S(2)}) copy-start(f32[24,16,256]{2,1,0:T(8,128)} %param.35) | copy-start | bytes 1179652
  31.8 15.1 %copy-start.15 = (f32[256]{0:T(256)S(1)}, f32[256]{0:T(256)}, u32[]{:S(2)}) copy-start(f32[256]{0:T(256)} %param.34) | copy-start | bytes 3076
  52.9 6.3 %copy-start.5 = (bf16[24,128]{1,0:T(8,128)(2,1)S(1)}, bf16[24,128]{1,0:T(8,128)(2,1)}, u32[]{:S(2)}) copy-start(bf16[24,128]{1,0:T(8,128)(2,1)} %hidden_ref.1) | copy-start | bytes 18436
